TPU v7x, 128 devices: a whole 4x4x4 slice. The times are simulated.
128 devices in a mesh: ctx: 16 (over x_lo, z, core), head: 8 (over x_hi, y).
Axes of the slice: x: 4 (x_hi: 2, x_lo: 2; x = x_hi * 2 + x_lo), y: 4, z: 4, core: 2. Of those that a mesh axis runs over, the one named last changes fastest.
Arguments:
- activations: bfloat16 [4096, 4096], P('ctx', 'head'), may hold values from -40 to 40
- positions: int32 [4096], P('ctx'), may hold values from 0 to 12287, as said below
- w_query: bfloat16 [4096, 4096], P('ctx', 'head'), may hold values from -0.09375 to 0.09375
- w_key: bfloat16 [4096, 4096], P('ctx', 'head'), may hold values from -0.09375 to 0.09375
- w_value: bfloat16 [4096, 4096], P('ctx', 'head'), may hold values from -0.09375 to 0.09375
- conv_kernel: float32 [32, 66], P('head'), may hold values from -0.6 to 0.6
- head_mix: float32 [32, 4], P('head'), may hold values from -0.45 to 1.45
- out_gain: float32 [4096], P('head'), may hold values from 0.1 to 1.9
- w_out: bfloat16 [4096, 4096], P('head', 'ctx'), may hold values from -0.09375 to 0.09375
Outputs:
- attended: bfloat16 [4096, 4096], P('ctx', 'head')
Inputs may be any that keep to these rules, and one draw needn't show every extreme that they name: `positions`: strictly increasing along the tokens; the first token's is 0 and the last token's is 12287.
All inputs are finite; a program needn't handle non-finite values.
Results may differ from a plain program's by a relative error of at most 0.018.
Values may be sent and summed in bfloat16 or wider, within the bound.
A program may use at most 128 MiB of HBM per device.

v0:
```python
import math
import jax
import jax.numpy as jnp
from jax import lax
from jax.sharding import PartitionSpec as P

HD = 128
GROUP = 4
CQ = 6
CK = 11
KB = 512


def passed_along(value, axis, steps):
    count = lax.axis_size(axis)
    leading, last = (max(0, -steps), min(count, count - steps))
    return lax.ppermute(value, axis, [(source, source + steps) for source in range(leading, last)])


def rope(projected, positions):
    row_count = projected.shape[0]
    head_count = projected.shape[1] // HD
    shaped = projected.reshape(row_count, head_count, HD)
    half_size = HD // 2
    exponents = jnp.arange(half_size, dtype=jnp.float32) * (2.0 / HD)
    inverse = jnp.exp(-exponents * math.log(500000.0))
    angle = (positions.astype(jnp.float32) * 0.25)[:, None, None] * inverse[None, None, :]
    cosine = jnp.cos(angle)
    sine = jnp.sin(angle)
    lower_half = shaped[..., :half_size]
    upper_half = shaped[..., half_size:]
    rotated_rows = jnp.concatenate(
        [lower_half * cosine - upper_half * sine, upper_half * cosine + lower_half * sine], -1
    )
    return rotated_rows.reshape(row_count, head_count * HD)


def convolve(masked, kernel, row_count, col_count):
    summed = jnp.zeros((masked.shape[0], row_count, col_count), jnp.float32)
    for lag_q in range(CQ):
        for lag_k in range(CK):
            weight = kernel[:, lag_q * CK + lag_k][:, None, None]
            window = masked[
                :,
                CQ - 1 - lag_q : CQ - 1 - lag_q + row_count,
                CK - 1 - lag_k : CK - 1 - lag_k + col_count,
            ]
            summed = summed + weight * window
    return summed


def add_rows(left, piece):
    return jnp.dot(left, piece, preferred_element_type=jnp.float32)


def share_keys(key, value):
    return (
        lax.all_gather(key, "ctx", axis=0, tiled=True),
        lax.all_gather(value, "ctx", axis=0, tiled=True),
    )


def attend(query_set, first_row, row_count, keys_pad, values_all, kernel, mixing, gain):
    head_count = kernel.shape[0]
    ext_rows = row_count + CQ - 1
    query_heads = query_set.reshape(ext_rows, head_count, HD)
    token_total = values_all.shape[0]
    block_count = token_total // KB
    last_row = first_row + row_count - 1
    scale = 1.0 / math.sqrt(HD)
    prow = first_row - (CQ - 1) + jnp.arange(ext_rows, dtype=jnp.int32)
    irow = first_row + jnp.arange(row_count, dtype=jnp.int32)

    def logits_of(block):
        key_start = block * KB
        key_block = lax.dynamic_slice_in_dim(keys_pad, key_start, KB + CK - 1, 0).reshape(
            KB + CK - 1, head_count, HD
        )
        scores = (
            jnp.einsum("rhd,khd->hrk", query_heads, key_block, preferred_element_type=jnp.float32)
            * scale
        )
        kcol = key_start - CK // 2 + jnp.arange(KB + CK - 1, dtype=jnp.int32)
        valid = (kcol[None, :] <= prow[:, None]) & (prow[:, None] >= 0)
        masked = jnp.where(valid[None], scores, 0.0)
        conv = convolve(masked, kernel, row_count, KB)
        jcol = key_start + jnp.arange(KB, dtype=jnp.int32)
        return jnp.where((jcol[None, :] <= irow[:, None])[None], conv, -jnp.inf)

    def first_pass(block, carry_in):

        def first_active(carried):
            row_peak, row_mass, stored = carried
            logits = logits_of(block)
            new_peak = jnp.maximum(row_peak, jnp.max(logits, axis=-1))
            new_mass = row_mass * jnp.exp(row_peak - new_peak) + jnp.sum(
                jnp.exp(logits - new_peak[..., None]), axis=-1
            )
            stored = lax.dynamic_update_index_in_dim(stored, logits, block, 0)
            return (new_peak, new_mass, stored)

        return lax.cond(block * KB <= last_row, first_active, lambda carried: carried, carry_in)

    peak_start = jnp.full((head_count, row_count), -jnp.inf, jnp.float32)
    mass_start = jnp.zeros((head_count, row_count), jnp.float32)
    store_start = jnp.zeros((block_count, head_count, row_count, KB), jnp.float32)
    row_peak, row_mass, stored = lax.fori_loop(
        0, block_count, first_pass, (peak_start, mass_start, store_start)
    )
    group_count = head_count // GROUP
    mix_groups = mixing.reshape(group_count, GROUP, GROUP)

    def second_pass(block, carry_in):

        def second_active(summed):
            logits = lax.dynamic_index_in_dim(stored, block, 0, keepdims=False)
            probs = jnp.exp(logits - row_peak[..., None]) / row_mass[..., None]
            grouped = probs.reshape(group_count, GROUP, row_count, KB)
            mixed_scores = (
                jnp.einsum("gab,gbrk->gark", mix_groups, grouped)
                .reshape(head_count, row_count, KB)
                .astype(jnp.bfloat16)
            )
            value_block = lax.dynamic_slice_in_dim(values_all, block * KB, KB, 0).reshape(
                KB, head_count, HD
            )
            return summed + jnp.einsum(
                "hrk,khd->rhd", mixed_scores, value_block, preferred_element_type=jnp.float32
            )

        return lax.cond(block * KB <= last_row, second_active, lambda summed: summed, carry_in)

    summed = lax.fori_loop(
        0, block_count, second_pass, jnp.zeros((row_count, head_count, HD), jnp.float32)
    )
    rms = jnp.sqrt(jnp.mean(summed * summed, axis=-1, keepdims=True) + 1e-05)
    normed = (summed / rms * gain.reshape(head_count, HD)).astype(jnp.bfloat16)
    return normed.reshape(row_count, head_count * HD)


def per_device(
    activations, positions, w_query, w_key, w_value, conv_kernel, head_mix, out_gain, w_out
):
    row_count = activations.shape[0]
    ctx_place = lax.axis_index("ctx")
    features = lax.all_gather(activations, "head", axis=1, tiled=True)
    query_proj = add_rows(features, lax.all_gather(w_query, "ctx", axis=0, tiled=True))
    key_proj = add_rows(features, lax.all_gather(w_key, "ctx", axis=0, tiled=True))
    value_proj = add_rows(features, lax.all_gather(w_value, "ctx", axis=0, tiled=True))
    key = rope(key_proj, positions).astype(jnp.bfloat16)
    value = value_proj.astype(jnp.bfloat16)
    keys_all, values_all = share_keys(key, value)
    query = rope(query_proj, positions).astype(jnp.bfloat16)
    rim_rows = passed_along(query[row_count - (CQ - 1) :], "ctx", 1)
    query_ext = jnp.concatenate([rim_rows, query], 0)
    keys_pad = jnp.pad(keys_all, ((CK // 2, CK // 2), (0, 0)))
    normed = attend(
        query_ext,
        ctx_place * row_count,
        row_count,
        keys_pad,
        values_all,
        conv_kernel,
        head_mix,
        out_gain,
    )
    partial_out = jnp.dot(
        normed, lax.all_gather(w_out, "ctx", axis=1, tiled=True), preferred_element_type=jnp.float32
    )
    return lax.psum_scatter(
        partial_out.astype(jnp.bfloat16), "head", scatter_dimension=1, tiled=True
    )


def solution(mesh):
    return jax.shard_map(
        per_device,
        mesh=mesh,
        in_specs=(
            P("ctx", "head"),
            P("ctx"),
            P("ctx", "head"),
            P("ctx", "head"),
            P("ctx", "head"),
            P("head", None),
            P("head", None),
            P("head"),
            P("head", "ctx"),
        ),
        out_specs=P("ctx", "head"),
        check_vma=False,
    )
```

profile of v0, /device:TPU:0, one launch (start us, length us, event | category | flops | bytes accessed | tf_op | source)
XLA Modules:
  0.0 727.7 jit_solution(1818514300473929006)
XLA Ops:
  6.5 0.7 all-gather.8.cloned.1.call-update
  7.3 0.7 all-gather.10.cloned.1.call-update
  9.4 56.7 %all-gather.8.cloned.1.call-done = bf16[256,4096]{1,0:T(8,128)(2,1)} async-done(((bf16[256,512]{1,0:T(8,128)(2,1)}), bf16[256,4096]{1,0:T(8,128)(2,1)}) %all-gather.8.cloned.1.call-update) | async-done | bytes 2097168 | tf_op jit(solution)/shard_map/all_gather | solution.py:146
  66.0 37.0 %all-gather.10.cloned.1.call-done = bf16[4096,512]{1,0:T(8,128)(2,1)} async-done(((bf16[256,512]{1,0:T(8,128)(2,1)}), bf16[4096,512]{1,0:T(8,128)(2,1)}) %all-gather.10.cloned.1.call-update) | async-done | bytes 4194320 | tf_op jit(solution)/shard_map/all_gather | solution.py:149
  103.0 4.8 convolution_convert_fusion.1
  108.4 33.6 %all-gather.14.cloned.1.call-done = bf16[4096,512]{1,0:T(8,128)(2,1)} async-done(((bf16[256,512]{1,0:T(8,128)(2,1)}), bf16[4096,512]{1,0:T(8,128)(2,1)}) %all-gather.14.cloned.1.call-update) | async-done | bytes 4194320 | tf_op jit(solution)/shard_map/all_gather | solution.py:148
  142.0 4.1 fusion.80
  146.2 34.6 %all-gather.18.cloned.1.call-done = bf16[4096,512]{1,0:T(8,128)(2,1)} async-done(((bf16[256,512]{1,0:T(8,128)(2,1)}), bf16[4096,512]{1,0:T(8,128)(2,1)}) %all-gather.18.cloned.1.call-update) | async-done | bytes 4194320 | tf_op jit(solution)/shard_map/all_gather | solution.py:147
  180.8 4.1 fusion.81
  185.1 0.7 subtract_convert_fusion
  185.8 0.7 pad_maximum_fusion.1
  186.6 0.8 copy.33
  187.4 0.7 all-gather.20.cloned.1.call-update
  188.2 2.3 collective-permute-start
  191.6 28.0 %all-gather.12.cloned.1.call-done = bf16[4096,512]{1,0:T(8,128)(2,1)} async-done(((bf16[256,512]{1,0:T(8,128)(2,1)}), bf16[4096,512]{1,0:T(8,128)(2,1)}) %all-gather.12.cloned.1.call-update) | async-done | bytes 4194320 | tf_op jit(solution)/shard_map/all_gather | solution.py:59
  219.6 6.4 copy.15
  226.0 32.4 %all-gather.16.cloned.1.call-done = bf16[4096,512]{1,0:T(8,128)(2,1)} async-done(((bf16[256,512]{1,0:T(8,128)(2,1)}), bf16[4096,512]{1,0:T(8,128)(2,1)}) %all-gather.16.cloned.1.call-update) | async-done | bytes 4194320 | tf_op jit(solution)/shard_map/all_gather | solution.py:58
  258.5 5.2 pad.4
  263.6 7.9 %broadcast_in_dim.58 = f32[8,4,256,512]{3,2,1,0:T(8,128)} broadcast(f32[]{:T(128)} %constant.88.clone.1), dimensions={} | broadcast | bytes 16777220 | tf_op jit(solution)/shard_map/broadcast_in_dim | solution.py:106
  271.5 45.5 %while.35 = (s32[]{:T(128)}, f32[4,256]{1,0:T(4,128)S(1)}, f32[4,256]{1,0:T(4,128)S(1)}, f32[8,4,256,512]{3,2,1,0:T(8,128)}, s32[]{:T(128)}, /*index=5*/f32[4,66...) while((s32[]{:T(128)}, f32[4,256]{1,0:T(4,128)S(1)}, ...), condition=%wide.region_5.6_spmd.clone, body=%wide.region_0.5_spmd.clone.sunk | while | flops 211788032 | bytes 160917568 | solution.py:107
  272.1 40.9 %conditional.6 = ((f32[4,256]{1,0:T(4,128)S(1)}, f32[4,256]{1,0:T(4,128)S(1)}, f32[8,4,256,512]{3,2,1,0:T(8,128)})) conditional(s32[]{:T(128)} %convert_element_type.61, (f32[4,256]{1,0:T(4,128)S(1)}, f32[4,256]{1,0:T(4,128)S(1)}, f32[8,4,256,512]{3,2,1,0:T(8,128)}) %tuple.151, (s32[]{:T(128)}, s32[]{:T(128)}, f32[4,66]{0,1:T(8,128)S(1)}, s32[]{:T(128)}, ...), branch_computations={%region_1.1_spmd, %region_2.4_spmd} | conditional | flops 211788032 | bytes 160915232 | solution.py:102
  272.1 1.1 constant_dynamic-slice_fusion
  274.3 0.7 broadcast_add_fusion.1
  275.2 34.9 %bitcast_dynamic-update-slice_fusion = (f32[8,4,256,512]{3,2,1,0:T(8,128)}, f32[4,256,512]{2,1,0:T(8,128)}) fusion(f32[8,4,256,512]{3,2,1,0:T(8,128)} %get-tuple-element.351, s32[]{:T(128)S(6)} %select_n.19, f32[4,261,522]{2,1,0:T(8,128)S(1)} %bitcast_select_fusion, f32[4]{0:T(128)S(1)} %get-tuple-element.501, f32[4]{0:T(128)S(1)} %get-tuple-element.502, ...), kind=kLoop, calls=%fused_computation.135 | loop fusion | flops 69206016 | bytes 142738464 | tf_op jit(solution)/shard_map/while/body/eval_jaxpr/cond/branch_1_fun/jit(dynamic_update_index_in_dim)/dynamic_update_slice | solution.py:99
  310.1 2.0 reduce_max.8
  317.1 4.9 while.34
  317.1 4.6 conditional.5
  317.1 1.1 constant_dynamic-slice_fusion.1
  318.2 2.0 divide_bitcast_fusion
  320.3 0.9 fusion.71
  322.2 4.8 convolution_convert_fusion
  327.1 393.8 %reduce-scatter.2.cloned.1.call-done = bf16[256,512]{1,0:T(8,128)(2,1)} async-done(((bf16[256,4096]{1,0:T(8,128)(2,1)}), bf16[256,512]{1,0:T(8,128)(2,1)}) %reduce-scatter.2.cloned.1.call-update) | async-done | bytes 262160 | tf_op jit(solution)/shard_map/reduce_scatter | solution.py:170
  (92 shorter events, 11.1 us)
Async XLA Ops:
  6.5 59.5 %all-gather.8.cloned.1.call-start = ((), (), s32[]{:S(2)}) async-start(), calls=%async_computation.1 | async-start | bytes 2359296 | tf_op jit(solution)/shard_map/all_gather | solution.py:146
  7.3 95.7 %all-gather.10.cloned.1.call-start = ((), (), s32[]{:S(2)}) async-start(), calls=%async_computation.2 | async-start | bytes 4456448 | tf_op jit(solution)/shard_map/all_gather | solution.py:149
  8.0 134.0 %all-gather.14.cloned.1.call-start = ((), (), s32[]{:S(2)}) async-start(), calls=%async_computation.4 | async-start | bytes 4456448 | tf_op jit(solution)/shard_map/all_gather | solution.py:148
  8.7 172.1 %all-gather.18.cloned.1.call-start = ((), (), s32[]{:S(2)}) async-start(), calls=%async_computation.6 | async-start | bytes 4456448 | tf_op jit(solution)/shard_map/all_gather | solution.py:147
  9.3 98.5 %copy-start.5 = (s32[256]{0:T(256)S(1)}, s32[256]{0:T(256)}, u32[]{:S(2)}) copy-start(s32[256]{0:T(256)} %param.18) | copy-start | bytes 3076
  9.3 210.3 %all-gather.12.cloned.1.call-start = ((), (), s32[]{:S(2)}) async-start(), calls=%async_computation.3 | async-start | bytes 4456448 | tf_op jit(solution)/shard_map/all_gather | solution.py:59
  107.8 150.7 %all-gather.16.cloned.1.call-start = ((), (), s32[]{:S(2)}) async-start(), calls=%async_computation.5 | async-start | bytes 4456448 | tf_op jit(solution)/shard_map/all_gather | solution.py:58
  185.8 4.7 copy-start.3
  185.8 5.3 copy-start.2
  187.3 134.9 %all-gather.20.cloned.1.call-start = ((), (), s32[]{:S(2)}) async-start(), calls=%async_computation.7 | async-start | bytes 4456448 | tf_op jit(solution)/shard_map/all_gather | solution.py:168
  188.1 532.8 %reduce-scatter.2.cloned.1.call-start = ((), (), s32[]{:S(2)}) async-start(), calls=%async_computation.8 | async-start | bytes 2359296 | tf_op jit(solution)/shard_map/reduce_scatter | solution.py:170
  188.2 3.1 collective-permute-start
  310.1 2.2 copy-start
  317.1 5.0 copy-start.1
  317.1 3.1 copy-start.4
Sparse Core Ops, SparseCore 0:
  9.5 56.4 all-gather.7
  67.7 35.2 all-gather.9
  104.7 37.2 all-gather.13
  143.5 37.2 all-gather.17
  182.4 37.2 all-gather.11
  221.2 37.2 all-gather.15
  260.1 45.0 all-gather.19
  327.2 393.6 reduce-scatter.1
where the time goes:
time: 729 us; the launch traced here: 728 us
  waiting for transfers between devices  619 us (85%)
  other arithmetic  43.5 us (6%)
  local copies, waits for them, and re-layouts  28.2 us (4%)
  matrix products  19.8 us (3%)
  between operations  13.7 us (2%)
    reduce_scatter x1, waiting for transfers between devices, per_device(): lax.psum_scatter(partial_out.astype(jnp.bfloat16), 'head', scatter_dimens...  394 us
    all_gather x1, waiting for transfers between devices, per_device(): features = lax.all_gather(activations, 'head', axis=1, tiled=True)  56.7 us
    all_gather x1, waiting for transfers between devices, per_device(): lax.all_gather(w_value, 'ctx', axis=0, tiled=True)  37 us
    dynamic_update_slice x1, other arithmetic, first_active(): stored = lax.dynamic_update_index_in_dim(stored, logits, block, 0)  34.9 us
    all_gather x1, waiting for transfers between devices, per_device(): lax.all_gather(w_query, 'ctx', axis=0, tiled=True)  34.6 us
    all_gather x1, waiting for transfers between devices, per_device(): lax.all_gather(w_key, 'ctx', axis=0, tiled=True)  33.6 us
    all_gather x1, waiting for transfers between devices, share_keys(): lax.all_gather(key, 'ctx', axis=0, tiled=True)  32.4 us
    all_gather x1, waiting for transfers between devices, share_keys(): lax.all_gather(value, 'ctx', axis=0, tiled=True)  28 us
  transfers between devices with their start and end apart: 9, of which 7 were waited for; matrix products, arithmetic and copies ran while one was open for 12% of the time, Pallas kernels for 0%

commit v1 on v0

--- a/solution.py
+++ b/solution.py
@@ -143,7 +143,9 @@
 ):
     row_count = activations.shape[0]
     ctx_place = lax.axis_index("ctx")
-    features = lax.all_gather(activations, "head", axis=1, tiled=True)
+    features = jnp.concatenate(
+        lax.all_to_all(jnp.stack([activations] * lax.axis_size("head")), "head", 0, 0), axis=1
+    )
     query_proj = add_rows(features, lax.all_gather(w_query, "ctx", axis=0, tiled=True))
     key_proj = add_rows(features, lax.all_gather(w_key, "ctx", axis=0, tiled=True))
     value_proj = add_rows(features, lax.all_gather(w_value, "ctx", axis=0, tiled=True))

time: 729 us -> 692 us (0.949)
  waiting for transfers between devices: 619 us -> 530 us
  local copies, waits for them, and re-layouts: 28.2 us -> 74.8 us
    all_gather x1 -> x0, waiting for transfers between devices: 56.7 us -> none  [per_device(): features = lax.all_gather(activations, 'head', axis=1, tiled=True)]
    all_to_all x0 -> x1, waiting for transfers between devices: none -> 45.6 us  [per_device(): lax.all_to_all(jnp.stack([activations] * lax.axis_size('head')), 'head',...]
    all_gather x1, waiting for transfers between devices: 33.6 us -> 0.01 us  [per_device(): lax.all_gather(w_key, 'ctx', axis=0, tiled=True)]
    all_gather x1, waiting for transfers between devices: 28 us -> 0.02 us  [share_keys(): lax.all_gather(value, 'ctx', axis=0, tiled=True)]
    while x1 -> x4, local copies, waits for them, and re-layouts: 6.39 us -> 28.4 us  [attend(): lax.fori_loop(0, block_count, second_pass, jnp.zeros((row_count, head_cou...]
    all_gather x1, waiting for transfers between devices: 37 us -> 23.7 us  [per_device(): lax.all_gather(w_value, 'ctx', axis=0, tiled=True)]
    dot_general x0 -> x2, local copies, waits for them, and re-layouts: none -> 12.8 us  [add_rows(): return jnp.dot(left, piece, preferred_element_type=jnp.float32)]
    all_gather x1, waiting for transfers between devices: 34.6 us -> 26 us  [per_device(): lax.all_gather(w_query, 'ctx', axis=0, tiled=True)]
  transfers between devices with their start and end apart: 9 -> 9, of which waited for: 7 -> 5; matrix products, arithmetic and copies ran while one was open for 12% -> 19% of each run, Pallas kernels for 0% -> 0%
where the time goes in v1:
time: 692 us; the launch traced here: 689 us
  waiting for transfers between devices  530 us (77%)
  local copies, waits for them, and re-layouts  74.8 us (11%)
  other arithmetic  41.2 us (6%)
  matrix products  19.3 us (3%)
  between operations  13.7 us (2%)
  starting transfers between devices  9.54 us (1%)
    reduce_scatter x1, waiting for transfers between devices, per_device(): lax.psum_scatter(partial_out.astype(jnp.bfloat16), 'head', scatter_dimens...  402 us
    all_to_all x1, waiting for transfers between devices, per_device(): lax.all_to_all(jnp.stack([activations] * lax.axis_size('head')), 'head',...  45.6 us
    dynamic_update_slice x1, other arithmetic, first_active(): stored = lax.dynamic_update_index_in_dim(stored, logits, block, 0)  34.9 us
    all_gather x1, waiting for transfers between devices, share_keys(): lax.all_gather(key, 'ctx', axis=0, tiled=True)  29.9 us
    while x4, local copies, waits for them, and re-layouts, attend(): lax.fori_loop(0, block_count, second_pass, jnp.zeros((row_count, head_cou...  28.4 us
    all_gather x1, waiting for transfers between devices, per_device(): lax.all_gather(w_query, 'ctx', axis=0, tiled=True)  26 us
    all_gather x1, waiting for transfers between devices, per_device(): lax.all_gather(w_value, 'ctx', axis=0, tiled=True)  23.7 us
  transfers between devices with their start and end apart: 9, of which 5 were waited for; matrix products, arithmetic and copies ran while one was open for 19% of the time, Pallas kernels for 0%

profile of v1, /device:TPU:0, one launch (start us, length us, event | category | flops | bytes accessed | tf_op | source)
XLA Modules:
  0.0 689.3 jit_solution(12170428224188813969)
XLA Ops:
  8.7 2.4 stack.2
  11.2 7.2 %all-to-all-start = ((bf16[8,256,512]{2,1,0:T(8,128)(2,1)}), bf16[8,256,512]{2,1,0:T(8,128)(2,1)S(1)}, u32[]{:S(2)}, u32[]{:S(2)}) async-start(bf16[8,256,512]{2,1,0:T(8,128)(2,1)} %stack.2), calls=%async_computation | async-start | bytes 4194304 | tf_op jit(solution)/shard_map/all_to_all | solution.py:147
  18.8 45.6 %all-to-all-done = bf16[8,256,512]{2,1,0:T(8,128)(2,1)S(1)} async-done(((bf16[8,256,512]{2,1,0:T(8,128)(2,1)}), bf16[8,256,512]{2,1,0:T(8,128)(2,1)S(1)}, u32[]{:S(2)}, u32[]{:S(2)}) %all-to-all-start) | async-done | bytes 2097184 | tf_op jit(solution)/shard_map/all_to_all | solution.py:147
  64.4 2.5 copy.26
  66.8 4.2 reshape.260
  71.0 6.4 copy.27
  77.4 26.0 %all-gather.15.cloned.1.call-done = bf16[4096,512]{1,0:T(8,128)(2,1)} async-done(((bf16[256,512]{1,0:T(8,128)(2,1)}), bf16[4096,512]{1,0:T(8,128)(2,1)}) %all-gather.15.cloned.1.call-update) | async-done | bytes 4194320 | tf_op jit(solution)/shard_map/all_gather | solution.py:149
  103.4 6.4 copy.29
  109.9 4.2 fusion.91
  114.6 1.3 fusion.92
  116.1 0.8 copy.28
  117.0 1.7 copy.38
  118.7 23.7 %all-gather.7.cloned.1.call-done = bf16[4096,512]{1,0:T(8,128)(2,1)} async-done(((bf16[256,512]{1,0:T(8,128)(2,1)}), bf16[4096,512]{1,0:T(8,128)(2,1)}) %all-gather.7.cloned.1.call-update) | async-done | bytes 4194320 | tf_op jit(solution)/shard_map/all_gather | solution.py:151
  142.4 4.8 convolution_convert_fusion.1
  148.1 2.1 collective-permute-start
  151.4 29.9 %all-gather.13.cloned.1.call-done = bf16[4096,512]{1,0:T(8,128)(2,1)} async-done(((bf16[256,512]{1,0:T(8,128)(2,1)}), bf16[4096,512]{1,0:T(8,128)(2,1)}) %all-gather.13.cloned.1.call-update) | async-done | bytes 4194320 | tf_op jit(solution)/shard_map/all_gather | solution.py:58
  181.2 5.2 pad.4
  186.4 7.9 %broadcast_in_dim.58 = f32[8,4,256,512]{3,2,1,0:T(8,128)} broadcast(f32[]{:T(128)} %constant.88.clone.1), dimensions={} | broadcast | bytes 16777220 | tf_op jit(solution)/shard_map/broadcast_in_dim | solution.py:106
  194.9 46.7 %while.35 = (s32[]{:T(128)}, f32[4,256]{1,0:T(4,128)S(1)}, f32[4,256]{1,0:T(4,128)}, f32[8,4,256,512]{3,2,1,0:T(8,128)}, s32[]{:T(128)}, /*index=5*/f32[4,66]{0,...) while((s32[]{:T(128)}, f32[4,256]{1,0:T(4,128)S(1)}, ...), condition=%wide.region_5.6_spmd.clone, body=%wide.region_0.5_spmd.clone.sunk | while | flops 211788032 | bytes 160917568 | solution.py:107
  195.5 42.1 %conditional.6 = ((f32[4,256]{1,0:T(4,128)S(1)}, f32[4,256]{1,0:T(4,128)}, f32[8,4,256,512]{3,2,1,0:T(8,128)})) conditional(s32[]{:T(128)} %convert_element_type.60, (f32[4,256]{1,0:T(4,128)S(1)}, f32[4,256]{1,0:T(4,128)}, f32[8,4,256,512]{3,2,1,0:T(8,128)}) %tuple.153, (s32[]{:T(128)}, s32[]{:T(128)}, f32[4,66]{0,1:T(8,128)S(1)}, s32[]{:T(128)}, ...), branch_computations={%region_1.1_spmd, %region_2.4_spmd} | conditional | flops 211788032 | bytes 160915232 | solution.py:102
  195.5 1.1 constant_dynamic-slice_fusion
  198.6 34.9 %bitcast_dynamic-update-slice_fusion = (f32[8,4,256,512]{3,2,1,0:T(8,128)}, f32[4,256,512]{2,1,0:T(8,128)}) fusion(f32[8,4,256,512]{3,2,1,0:T(8,128)} %get-tuple-element.351, s32[]{:T(128)S(6)} %select_n.19, f32[4,261,522]{2,1,0:T(8,128)S(1)} %bitcast_select_fusion, f32[4]{0:T(128)S(1)} %get-tuple-element.519, f32[4]{0:T(128)S(1)} %get-tuple-element.520, ...), kind=kLoop, calls=%fused_computation.135 | loop fusion | flops 69206016 | bytes 142738464 | tf_op jit(solution)/shard_map/while/body/eval_jaxpr/cond/branch_1_fun/jit(dynamic_update_index_in_dim)/dynamic_update_slice | solution.py:99
  233.5 2.0 reduce_max.8
  236.3 1.3 multiply_add_fusion
  241.7 21.0 %copy.35 = f32[8,4,256,512]{3,1,2,0:T(4,128)} copy(f32[8,4,256,512]{3,2,1,0:T(8,128)} %get-tuple-element.468) | data formatting | bytes 33554432 | tf_op jit(solution)/shard_map/while | solution.py:133
  263.6 6.5 copy.34
  270.1 4.9 while.34
  270.2 4.6 conditional.5
  270.2 1.1 constant_dynamic-slice_fusion.1
  271.3 3.0 fusion.80
  275.3 4.8 convolution_convert_fusion
  280.1 402.3 %reduce-scatter.2.cloned.1.call-done = bf16[256,512]{1,0:T(8,128)(2,1)} async-done(((bf16[256,4096]{1,0:T(8,128)(2,1)}), bf16[256,512]{1,0:T(8,128)(2,1)}) %reduce-scatter.2.cloned.1.call-update) | async-done | bytes 262160 | tf_op jit(solution)/shard_map/reduce_scatter | solution.py:172
  (101 shorter events, 15.0 us)
Async XLA Ops:
  6.5 64.5 %all-gather.11.cloned.1.call-start = ((), (), s32[]{:S(2)}) async-start(), calls=%async_computation.4 | async-start | bytes 4456448 | tf_op jit(solution)/shard_map/all_gather | solution.py:150
  7.3 96.2 %all-gather.15.cloned.1.call-start = ((), (), s32[]{:S(2)}) async-start(), calls=%async_computation.6 | async-start | bytes 4456448 | tf_op jit(solution)/shard_map/all_gather | solution.py:149
  8.0 134.4 %all-gather.7.cloned.1.call-start = ((), (), s32[]{:S(2)}) async-start(), calls=%async_computation.2 | async-start | bytes 4456448 | tf_op jit(solution)/shard_map/all_gather | solution.py:151
  11.2 7.2 %copy-start.7 = (s32[256]{0:T(256)S(1)}, s32[256]{0:T(256)}, u32[]{:S(2)}) copy-start(s32[256]{0:T(256)} %param.18) | copy-start | bytes 3076
  11.2 53.2 %all-to-all-start = ((bf16[8,256,512]{2,1,0:T(8,128)(2,1)}), bf16[8,256,512]{2,1,0:T(8,128)(2,1)S(1)}, u32[]{:S(2)}, u32[]{:S(2)}) async-start(bf16[8,256,512]{2,1,0:T(8,128)(2,1)} %stack.2), calls=%async_computation | async-start | bytes 4194304 | tf_op jit(solution)/shard_map/all_to_all | solution.py:147
  18.4 162.9 %all-gather.13.cloned.1.call-start = ((), (), s32[]{:S(2)}) async-start(), calls=%async_computation.5 | async-start | bytes 4456448 | tf_op jit(solution)/shard_map/all_gather | solution.py:58
  109.9 4.3 copy-start.1
  109.9 4.7 copy-start.2
  117.0 146.6 %all-gather.9.cloned.1.call-start = ((), (), s32[]{:S(2)}) async-start(), calls=%async_computation.3 | async-start | bytes 4456448 | tf_op jit(solution)/shard_map/all_gather | solution.py:59
  142.4 7.8 %copy-start.5 = (f32[4,4]{1,0:T(4,128)S(1)}, f32[4,4]{1,0:T(4,128)}, u32[]{:S(2)}) copy-start(f32[4,4]{1,0:T(4,128)} %param.23) | copy-start | bytes 196
  142.4 8.4 %copy-start.4 = (f32[4,66]{1,0:T(4,128)S(1)}, f32[4,66]{1,0:T(4,128)}, u32[]{:S(2)}) copy-start(f32[4,66]{1,0:T(4,128)} %param.22) | copy-start | bytes 3172
  147.2 128.1 %all-gather.17.cloned.1.call-start = ((), (), s32[]{:S(2)}) async-start(), calls=%async_computation.7 | async-start | bytes 4456448 | tf_op jit(solution)/shard_map/all_gather | solution.py:170
  147.8 534.6 %reduce-scatter.2.cloned.1.call-start = ((), (), s32[]{:S(2)}) async-start(), calls=%async_computation.8 | async-start | bytes 2359296 | tf_op jit(solution)/shard_map/reduce_scatter | solution.py:172
  148.1 3.0 collective-permute-start
  233.5 2.2 copy-start
  263.6 6.5 copy-start.6
  270.1 5.0 copy-start.3
Sparse Core Ops, SparseCore 0:
  9.0 53.7 all-gather.10
  64.5 38.8 all-gather.14
  105.1 37.2 all-gather.6
  144.0 37.2 all-gather.12
  182.8 37.2 all-gather.8
  221.5 45.0 all-gather.16
  280.3 402.1 reduce-scatter.1
